TPU v7x, 512 devices: a whole 4x8x8 slice. The times are simulated.
512 devices in a mesh: ctx: 64 (over z, y_hi, core), exp: 8 (over x, y_lo).
Axes of the slice: x: 4, y: 8 (y_hi: 4, y_lo: 2; y = y_hi * 2 + y_lo), z: 8, core: 2. Of those that a mesh axis runs over, the one named last changes fastest.
Arguments:
- residual: bfloat16 [4096, 2048], P('ctx', 'exp'), may hold values from -60 to 60
- queries: bfloat16 [4096, 2048], P('ctx', 'exp'), may hold values from -6.5 to 6.5
- keys: bfloat16 [4096, 2048], P('ctx', 'exp'), may hold values from -6.5 to 6.5
- values: bfloat16 [4096, 2048], P('ctx', 'exp'), may hold values from -6 to 6
- out_proj: bfloat16 [2048, 2048], P(None, 'exp'), may hold values from -0.5 to 0.5
- norm_gain: float32 [2048], replicated, may hold values from 0.1 to 1.9
- w_gate: bfloat16 [8, 2048, 8192], P('exp', None, 'ctx'), may hold values from -0.125 to 0.125
- w_up: bfloat16 [8, 2048, 8192], P('exp', None, 'ctx'), may hold values from -0.125 to 0.125
- w_down: bfloat16 [8, 8192, 2048], P('exp', 'ctx'), may hold values from -0.0625 to 0.0625
- routes: int32 [4096, 1], P('ctx'), may hold values from 0 to 7; in each aligned block of 64 rows (0 to 63, 64 to 127, ...) at most 8 rows name the same one
- block_mask: int32 [32, 32], replicated, may hold values from 0 to 1, as said below
Outputs:
- mixed: bfloat16 [8, 512, 2048], P('exp', 'ctx')
Inputs may be any that keep to these rules, and one draw needn't show every extreme that they name: `routes`: each stored row is named by exactly 8 of the 64 rows of one index of ctx. `block_mask`: every diagonal entry is 1.
All inputs are finite; a program needn't handle non-finite values.
Results may differ from a plain program's by a relative error of at most 0.006.
Values may be sent and summed in bfloat16 or wider, within the bound.
A program may use at most 64 MiB of HBM per device.

v0:
```python
import math
import jax
import jax.numpy as jnp
from jax import lax
from jax.sharding import PartitionSpec as P

HD = 128
BLK = 128


def body(
    residual, queries, keys, values, out_proj, norm_gain, w_gate, w_up, w_down, routes, block_mask
):
    local_tokens = residual.shape[0]
    local_width = queries.shape[1]
    heads_here = local_width // HD
    blocks_all = block_mask.shape[0]
    expert_count = lax.axis_size("exp")
    per_expert = local_tokens // expert_count
    scaling = 1.0 / math.sqrt(HD)
    ctx_place = lax.axis_index("ctx")
    query_pos = ctx_place * local_tokens + jnp.arange(local_tokens, dtype=jnp.int32)
    query_blocks = jax.nn.one_hot(query_pos // BLK, blocks_all, dtype=jnp.float32)
    query_mask = jnp.dot(query_blocks, block_mask.astype(jnp.float32))
    query_three = queries.reshape(local_tokens, heads_here, HD)
    key_piece = lax.all_gather(keys, "ctx", axis=0, tiled=True)
    value_piece = lax.all_gather(values, "ctx", axis=0, tiled=True)
    count_here = key_piece.shape[0]
    key_pos = jnp.arange(count_here, dtype=jnp.int32)
    key_blocks = jax.nn.one_hot(key_pos // BLK, blocks_all, dtype=jnp.float32)
    allowed = jnp.dot(query_mask, key_blocks.T) > 0.5
    top_old = jnp.full((heads_here, local_tokens), -1e30, jnp.float32)
    key_three = key_piece.reshape(count_here, heads_here, HD)
    value_three = value_piece.reshape(count_here, heads_here, HD)
    scores = (
        jnp.einsum("qhd,khd->hqk", query_three, key_three, preferred_element_type=jnp.float32)
        * scaling
    )
    scores = jnp.where(allowed[None], scores, -1e30)
    top_new = jnp.maximum(top_old, jnp.max(scores, axis=2))
    exponent = jnp.where(allowed[None], jnp.exp(scores - top_new[:, :, None]), 0.0)
    total_new = jnp.sum(exponent, axis=2)
    product = jnp.einsum(
        "hqk,khd->hqd",
        exponent.astype(jnp.bfloat16),
        value_three,
        preferred_element_type=jnp.float32,
    )
    attended = (product / total_new[:, :, None]).astype(jnp.bfloat16)
    attended = attended.transpose(1, 0, 2).reshape(local_tokens, local_width)
    projected = jnp.dot(
        lax.all_gather(attended, "exp", axis=1, tiled=True),
        out_proj,
        preferred_element_type=jnp.float32,
    )
    hidden = (residual.astype(jnp.float32) + projected).astype(jnp.bfloat16)
    target = routes[:, 0]
    token_ids = jnp.arange(local_tokens, dtype=jnp.int32)
    earlier = (target[:, None] == target[None, :]) & (token_ids[None, :] < token_ids[:, None])
    ranking = jnp.sum(earlier.astype(jnp.int32), axis=1)
    slot_of = target * per_expert + ranking
    slot_ids = jnp.arange(expert_count * per_expert, dtype=jnp.int32)
    placing = (slot_of[None, :] == slot_ids[:, None]).astype(jnp.bfloat16)
    send_buffer = jnp.dot(placing, hidden, preferred_element_type=jnp.float32).astype(jnp.bfloat16)
    send_buffer = send_buffer.reshape(expert_count, per_expert, hidden.shape[1])
    own_rows = lax.all_to_all(send_buffer, "exp", split_axis=0, concat_axis=2, tiled=True)[0]
    values_f = own_rows.astype(jnp.float32)
    meansq = jnp.mean(values_f * values_f, axis=1, keepdims=True)
    normed_own = (values_f * lax.rsqrt(meansq + 1e-05) * norm_gain).astype(jnp.bfloat16)
    normed_rows = lax.all_gather(normed_own, "ctx", axis=0, tiled=True)
    gate_v = jnp.dot(normed_rows, w_gate[0], preferred_element_type=jnp.float32)
    up_v = jnp.dot(normed_rows, w_up[0], preferred_element_type=jnp.float32)
    activ = (jax.nn.silu(gate_v) * up_v).astype(jnp.bfloat16)
    terms = jnp.dot(activ, w_down[0], preferred_element_type=jnp.float32)
    summed = lax.psum_scatter(terms, "ctx", scatter_dimension=0, tiled=True)
    return (own_rows.astype(jnp.float32) + summed).astype(jnp.bfloat16)[None]


def solution(mesh):
    in_specs = (
        P("ctx", "exp"),
        P("ctx", "exp"),
        P("ctx", "exp"),
        P("ctx", "exp"),
        P(None, "exp"),
        P(),
        P("exp", None, "ctx"),
        P("exp", None, "ctx"),
        P("exp", "ctx", None),
        P("ctx", None),
        P(),
    )
    out_specs = P("exp", "ctx", None)
    return jax.shard_map(body, mesh=mesh, in_specs=in_specs, out_specs=out_specs, check_vma=False)
```

profile of v0, /device:TPU:2, one launch (start us, length us, event | category | flops | bytes accessed | tf_op | source)
XLA Modules:
  0.0 478.8 jit_solution(12788094995489610600)
XLA Ops:
  6.5 0.0 copy-start
  6.5 0.0 all-gather.4.cloned.1.call-start
  6.5 0.7 all-gather.4.cloned.1.call-update
  7.3 0.0 all-gather.6.cloned.1.call-start
  7.3 0.7 all-gather.6.cloned.1.call-update
  8.0 0.0 all-gather.8.cloned.1.call-start
  8.1 0.9 convert_reduce_fusion
  9.0 0.7 multiply_add_fusion
  9.7 1.3 convolution_compare_fusion
  10.9 0.0 copy-start.3
  10.9 89.1 %all-gather.4.cloned.1.call-done = bf16[4096,256]{1,0:T(8,128)(2,1)} async-done(((bf16[64,256]{1,0:T(8,128)(2,1)}), bf16[4096,256]{1,0:T(8,128)(2,1)}) %all-gather.4.cloned.1.call-update) | async-done | bytes 2097168 | tf_op jit(solution)/shard_map/all_gather | solution.py:26
  100.0 4.1 copy.25
  104.1 2.4 fusion.43
  106.5 0.7 fusion.1
  107.1 76.6 %all-gather.6.cloned.1.call-done = bf16[4096,256]{1,0:T(8,128)(2,1)} async-done(((bf16[64,256]{1,0:T(8,128)(2,1)}), bf16[4096,256]{1,0:T(8,128)(2,1)}) %all-gather.6.cloned.1.call-update) | async-done | bytes 2097168 | tf_op jit(solution)/shard_map/all_gather | solution.py:27
  183.7 4.1 copy.28
  187.8 2.5 fusion.8
  190.3 26.8 %all_gather.14 = bf16[64,2048]{1,0:T(8,128)(2,1)S(1)} all-gather(bf16[64,256]{1,0:T(8,128)(2,1)S(1)} %bitcast.56), channel_id=1, replica_groups=mesh['ctx'=64,'exp'=8] {'exp'}, dimensions={1}, use_global_device_ids=true | all-gather | bytes 294912 | tf_op jit(solution)/shard_map/all_gather | solution.py:52
  217.1 0.0 copy-done
  217.1 0.4 fusion.9
  217.5 11.1 %all_to_all.4 = bf16[8,8,256]{2,1,0:T(8,128)(2,1)S(1)} all-to-all(bf16[8,8,256]{2,1,0:T(8,128)(2,1)S(1)} %fusion.9), channel_id=1, replica_groups=mesh['ctx'=64,'exp'=8] {'exp'}, dimensions={0} | all-to-all | bytes 65536 | tf_op jit(solution)/shard_map/all_to_all | solution.py:66
  228.6 0.1 multiply_reduce_fusion
  228.8 0.7 multiply_convert_fusion
  229.5 0.0 all-gather.8.cloned.1.call-update
  229.5 0.0 reduce-scatter.2.cloned.1.call-start
  229.6 80.5 %all-gather.8.cloned.1.call-done = bf16[512,2048]{1,0:T(8,128)(2,1)} async-done(((bf16[8,2048]{1,0:T(8,128)(2,1)}), bf16[512,2048]{1,0:T(8,128)(2,1)}) %all-gather.8.cloned.1.call-update) | async-done | bytes 2097168 | tf_op jit(solution)/shard_map/all_gather | solution.py:70
  310.0 2.5 fusion.19
  312.6 0.0 copy-done.1
  312.6 5.4 %fusion.4 = f32[512,2048]{1,0:T(8,128)} fusion(bf16[512,2048]{1,0:T(8,128)(2,1)S(1)} %copy-done.1, bf16[1,128,2048]{2,1,0:T(8,128)(2,1)} %param.19, bf16[1,2048,128]{2,1,0:T(8,128)(2,1)} %param.18, f32[512,128]{1,0:T(8,128)S(1)} %fusion.19), kind=kOutput, calls=%fused_computation.8 | convolution fusion | flops 537264128 | bytes 7602176 | tf_op jit(solution)/shard_map/dot_general | solution.py:74
  318.0 0.0 reduce-scatter.2.cloned.1.call-update
  318.0 152.8 %reduce-scatter.2.cloned.1.call-done = f32[8,2048]{1,0:T(8,128)} async-done(((f32[512,2048]{1,0:T(8,128)}), f32[8,2048]{1,0:T(8,128)}) %reduce-scatter.2.cloned.1.call-update) | async-done | bytes 65552 | tf_op jit(solution)/shard_map/reduce_scatter | solution.py:75
  470.8 1.5 fusion.29
  (12 shorter events, 0.1 us)
Async XLA Ops:
  6.5 210.6 %copy-start = (bf16[2048,256]{1,0:T(8,128)(2,1)S(1)}, bf16[2048,256]{1,0:T(8,128)(2,1)}, u32[]{:S(2)}) copy-start(bf16[2048,256]{1,0:T(8,128)(2,1)} %param.15) | copy-start | bytes 3145732
  6.5 93.5 %all-gather.4.cloned.1.call-start = ((), (), s32[]{:S(2)}) async-start(), calls=%async_computation.2 | async-start | bytes 2129920 | tf_op jit(solution)/shard_map/all_gather | solution.py:26
  7.3 176.5 %all-gather.6.cloned.1.call-start = ((), (), s32[]{:S(2)}) async-start(), calls=%async_computation.3 | async-start | bytes 2129920 | tf_op jit(solution)/shard_map/all_gather | solution.py:27
  8.0 302.0 %all-gather.8.cloned.1.call-start = ((), (), s32[]{:S(2)}) async-start(), calls=%async_computation.4 | async-start | bytes 2129920 | tf_op jit(solution)/shard_map/all_gather | solution.py:70
  10.9 93.2 %copy-start.3 = (bf16[64,256]{1,0:T(8,128)(2,1)S(1)}, bf16[64,256]{1,0:T(8,128)(2,1)}, u32[]{:S(2)}) copy-start(bf16[64,256]{1,0:T(8,128)(2,1)} %param.12) | copy-start | bytes 98308
  187.8 29.3 %copy-start.2 = (bf16[64,256]{1,0:T(8,128)(2,1)S(1)}, bf16[64,256]{1,0:T(8,128)(2,1)}, u32[]{:S(2)}) copy-start(bf16[64,256]{1,0:T(8,128)(2,1)} %param.11) | copy-start | bytes 98308
  187.8 40.9 %copy-start.4 = (f32[2048]{0:T(1024)S(1)}, f32[2048]{0:T(1024)}, u32[]{:S(2)}) copy-start(f32[2048]{0:T(1024)} %param.16) | copy-start | bytes 24580
  229.5 241.3 %reduce-scatter.2.cloned.1.call-start = ((), (), s32[]{:S(2)}) async-start(), calls=%async_computation.5 | async-start | bytes 4259840 | tf_op jit(solution)/shard_map/reduce_scatter | solution.py:75
  310.0 2.5 copy-start.1
Sparse Core Ops, SparseCore 0:
  10.7 89.2 all-gather.3
  103.3 80.3 all-gather.5
  229.6 80.3 all-gather.7
  318.2 152.6 reduce-scatter.1
where the time goes:
time: 479 us
  waiting for transfers between devices  400 us (84%)
  blocking collectives  37.9 us (8%)
  matrix products  14.5 us (3%)
  between operations  13.2 us (3%)
  local copies, waits for them, and re-layouts  8.24 us (2%)
    reduce_scatter x1, waiting for transfers between devices, body(): summed = lax.psum_scatter(terms, 'ctx', scatter_dimension=0, tiled=True)  153 us
    all_gather x1, waiting for transfers between devices, body(): key_piece = lax.all_gather(keys, 'ctx', axis=0, tiled=True)  89.1 us
    all_gather x1, waiting for transfers between devices, body(): normed_rows = lax.all_gather(normed_own, 'ctx', axis=0, tiled=True)  80.5 us
    all_gather x1, waiting for transfers between devices, body(): value_piece = lax.all_gather(values, 'ctx', axis=0, tiled=True)  76.6 us
    all_gather x1, blocking collectives, body(): lax.all_gather(attended, 'exp', axis=1, tiled=True)  26.8 us
    all_to_all x1, blocking collectives, body(): lax.all_to_all(send_buffer, 'exp', split_axis=0, concat_axis=2, tiled=True)  11.1 us
  transfers between devices with their start and end apart: 4, of which 4 were waited for; matrix products, arithmetic and copies ran while one was open for 2% of the time, Pallas kernels for 0%

commit v1 on v0

--- a/solution.py
+++ b/solution.py
@@ -23,7 +23,9 @@
     query_blocks = jax.nn.one_hot(query_pos // BLK, blocks_all, dtype=jnp.float32)
     query_mask = jnp.dot(query_blocks, block_mask.astype(jnp.float32))
     query_three = queries.reshape(local_tokens, heads_here, HD)
-    key_piece = lax.all_gather(keys, "ctx", axis=0, tiled=True)
+    key_piece = jnp.concatenate(
+        lax.all_to_all(jnp.stack([keys for _ in range(lax.axis_size("ctx"))]), "ctx", 0, 0), axis=0
+    )
     value_piece = lax.all_gather(values, "ctx", axis=0, tiled=True)
     count_here = key_piece.shape[0]
     key_pos = jnp.arange(count_here, dtype=jnp.int32)

time: 479 us -> 428 us (0.89)
  the two profiles are of different devices: /device:TPU:2 before, /device:TPU:4 now
where the time goes in v1:
time: 428 us
  waiting for transfers between devices  335 us (78%)
  blocking collectives  37 us (9%)
  starting transfers between devices  16.8 us (4%)
  matrix products  14 us (3%)
  between operations  13.2 us (3%)
  local copies, waits for them, and re-layouts  8.6 us (2%)
    reduce_scatter x1, waiting for transfers between devices, body(): summed = lax.psum_scatter(terms, 'ctx', scatter_dimension=0, tiled=True)  153 us
    all_gather x1, waiting for transfers between devices, body(): normed_rows = lax.all_gather(normed_own, 'ctx', axis=0, tiled=True)  81.3 us
    all_to_all x1, waiting for transfers between devices, body(): lax.all_to_all(jnp.stack([keys for _ in range(lax.axis_size('ctx'))]), 'c...  65.5 us
    all_gather x1, waiting for transfers between devices, body(): value_piece = lax.all_gather(values, 'ctx', axis=0, tiled=True)  34.8 us
    all_gather x1, blocking collectives, body(): lax.all_gather(attended, 'exp', axis=1, tiled=True)  25.4 us
    all_to_all x1, starting transfers between devices, body(): lax.all_to_all(jnp.stack([keys for _ in range(lax.axis_size('ctx'))]), 'c...  16.7 us
    all_to_all x1, blocking collectives, body(): lax.all_to_all(send_buffer, 'exp', split_axis=0, concat_axis=2, tiled=True)  11.6 us
  transfers between devices with their start and end apart: 4, of which 4 were waited for; matrix products, arithmetic and copies ran while one was open for 1% of the time, Pallas kernels for 0%

profile of v1, /device:TPU:4, one launch (start us, length us, event | category | flops | bytes accessed | tf_op | source)
XLA Modules:
  0.0 428.0 jit_solution(17210845377181707493)
XLA Ops:
  6.5 2.4 stack.2
  8.9 16.7 %all-to-all-start = ((bf16[64,64,256]{2,1,0:T(8,128)(2,1)}), bf16[64,64,256]{2,1,0:T(8,128)(2,1)S(1)}, u32[]{:S(2)}, u32[]{:S(2)}) async-start(bf16[64,64,256]{2,1,0:T(8,128)(2,1)} %stack.2), calls=%async_computation | async-start | bytes 4194304 | tf_op jit(solution)/shard_map/all_to_all | solution.py:27
  25.7 0.0 all-gather.3.cloned.1.call-start
  25.7 0.7 all-gather.3.cloned.1.call-update
  26.4 0.0 all-gather.5.cloned.1.call-start
  26.5 0.2 convert_reduce_fusion
  26.7 0.5 convolution_compare_fusion
  27.2 0.0 copy-start.4
  27.3 65.5 %all-to-all-done = bf16[64,64,256]{2,1,0:T(8,128)(2,1)S(1)} async-done(((bf16[64,64,256]{2,1,0:T(8,128)(2,1)}), bf16[64,64,256]{2,1,0:T(8,128)(2,1)S(1)}, u32[]{:S(2)}, u32[]{:S(2)}) %all-to-all-start) | async-done | bytes 2097184 | tf_op jit(solution)/shard_map/all_to_all | solution.py:27
  92.8 2.0 reshape_reshape.3
  94.8 0.0 copy-done.4
  94.8 2.6 fusion.44
  97.4 0.7 fusion.2
  98.1 34.8 %all-gather.3.cloned.1.call-done = bf16[4096,256]{1,0:T(8,128)(2,1)} async-done(((bf16[64,256]{1,0:T(8,128)(2,1)}), bf16[4096,256]{1,0:T(8,128)(2,1)}) %all-gather.3.cloned.1.call-update) | async-done | bytes 2097168 | tf_op jit(solution)/shard_map/all_gather | solution.py:29
  132.9 4.1 copy.25
  137.0 2.5 fusion.9
  139.6 25.4 %all_gather.10 = bf16[64,2048]{1,0:T(8,128)(2,1)S(1)} all-gather(bf16[64,256]{1,0:T(8,128)(2,1)S(1)} %bitcast.53), channel_id=1, replica_groups=mesh['ctx'=64,'exp'=8] {'exp'}, dimensions={1}, use_global_device_ids=true | all-gather | bytes 294912 | tf_op jit(solution)/shard_map/all_gather | solution.py:54
  164.9 0.0 copy-done
  164.9 0.4 fusion.10
  165.4 11.6 %all_to_all.14 = bf16[8,8,256]{2,1,0:T(8,128)(2,1)S(1)} all-to-all(bf16[8,8,256]{2,1,0:T(8,128)(2,1)S(1)} %fusion.10), channel_id=1, replica_groups=mesh['ctx'=64,'exp'=8] {'exp'}, dimensions={0} | all-to-all | bytes 65536 | tf_op jit(solution)/shard_map/all_to_all | solution.py:68
  177.0 0.1 multiply_reduce_fusion
  177.1 0.0 copy-done.3
  177.1 0.7 multiply_convert_fusion
  177.8 0.0 all-gather.5.cloned.1.call-update
  177.9 0.0 reduce-scatter.2.cloned.1.call-start
  177.9 81.3 %all-gather.5.cloned.1.call-done = bf16[512,2048]{1,0:T(8,128)(2,1)} async-done(((bf16[8,2048]{1,0:T(8,128)(2,1)}), bf16[512,2048]{1,0:T(8,128)(2,1)}) %all-gather.5.cloned.1.call-update) | async-done | bytes 2097168 | tf_op jit(solution)/shard_map/all_gather | solution.py:72
  259.2 2.5 fusion.20
  261.8 0.0 copy-done.1
  261.8 5.4 %fusion.5 = f32[512,2048]{1,0:T(8,128)} fusion(bf16[512,2048]{1,0:T(8,128)(2,1)S(1)} %copy-done.1, bf16[1,128,2048]{2,1,0:T(8,128)(2,1)} %param.19, bf16[1,2048,128]{2,1,0:T(8,128)(2,1)} %param.18, f32[512,128]{1,0:T(8,128)S(1)} %fusion.20), kind=kOutput, calls=%fused_computation.9 | convolution fusion | flops 537264128 | bytes 7602176 | tf_op jit(solution)/shard_map/dot_general | solution.py:76
  267.2 0.0 reduce-scatter.2.cloned.1.call-update
  267.2 152.8 %reduce-scatter.2.cloned.1.call-done = f32[8,2048]{1,0:T(8,128)} async-done(((f32[512,2048]{1,0:T(8,128)}), f32[8,2048]{1,0:T(8,128)}) %reduce-scatter.2.cloned.1.call-update) | async-done | bytes 65552 | tf_op jit(solution)/shard_map/reduce_scatter | solution.py:77
  420.0 1.5 fusion.30
  (16 shorter events, 0.1 us)
Async XLA Ops:
  6.5 158.4 %copy-start = (bf16[2048,256]{1,0:T(8,128)(2,1)S(1)}, bf16[2048,256]{1,0:T(8,128)(2,1)}, u32[]{:S(2)}) copy-start(bf16[2048,256]{1,0:T(8,128)(2,1)} %param.15) | copy-start | bytes 3145732
  8.9 17.5 %copy-start.6 = (s32[64,1]{0,1:T(1,128)S(1)}, s32[64,1]{0,1:T(1,128)}, u32[]{:S(2)}) copy-start(s32[64,1]{0,1:T(1,128)} %param.20) | copy-start | bytes 772
  8.9 17.7 %copy-start.5 = (s32[32,32]{1,0:T(8,128)S(1)}, s32[32,32]{1,0:T(8,128)}, u32[]{:S(2)}) copy-start(s32[32,32]{1,0:T(8,128)} %param.21) | copy-start | bytes 12292
  8.9 83.8 %all-to-all-start = ((bf16[64,64,256]{2,1,0:T(8,128)(2,1)}), bf16[64,64,256]{2,1,0:T(8,128)(2,1)S(1)}, u32[]{:S(2)}, u32[]{:S(2)}) async-start(bf16[64,64,256]{2,1,0:T(8,128)(2,1)} %stack.2), calls=%async_computation | async-start | bytes 4194304 | tf_op jit(solution)/shard_map/all_to_all | solution.py:27
  25.7 107.2 %all-gather.3.cloned.1.call-start = ((), (), s32[]{:S(2)}) async-start(), calls=%async_computation.3 | async-start | bytes 2129920 | tf_op jit(solution)/shard_map/all_gather | solution.py:29
  26.4 232.8 %all-gather.5.cloned.1.call-start = ((), (), s32[]{:S(2)}) async-start(), calls=%async_computation.4 | async-start | bytes 2129920 | tf_op jit(solution)/shard_map/all_gather | solution.py:72
  27.2 67.6 %copy-start.4 = (bf16[64,256]{1,0:T(8,128)(2,1)S(1)}, bf16[64,256]{1,0:T(8,128)(2,1)}, u32[]{:S(2)}) copy-start(bf16[64,256]{1,0:T(8,128)(2,1)} %param.12) | copy-start | bytes 98308
  137.0 27.9 %copy-start.2 = (bf16[64,256]{1,0:T(8,128)(2,1)S(1)}, bf16[64,256]{1,0:T(8,128)(2,1)}, u32[]{:S(2)}) copy-start(bf16[64,256]{1,0:T(8,128)(2,1)} %param.11) | copy-start | bytes 98308
  137.0 40.1 %copy-start.3 = (f32[2048]{0:T(1024)S(1)}, f32[2048]{0:T(1024)}, u32[]{:S(2)}) copy-start(f32[2048]{0:T(1024)} %param.16) | copy-start | bytes 24580
  177.9 242.1 %reduce-scatter.2.cloned.1.call-start = ((), (), s32[]{:S(2)}) async-start(), calls=%async_computation.5 | async-start | bytes 4259840 | tf_op jit(solution)/shard_map/reduce_scatter | solution.py:77
  259.2 2.5 copy-start.1
Sparse Core Ops, SparseCore 0:
  29.8 103.0 all-gather.2
  178.0 81.1 all-gather.4
  267.4 152.5 reduce-scatter.1
